TPU v7x, 256 devices: a whole 4x4x8 slice. The times are simulated.
256 devices in a mesh: seq: 128 (over z, y, x_lo, core), head: 2 (over x_hi).
Axes of the slice: x: 4 (x_hi: 2, x_lo: 2; x = x_hi * 2 + x_lo), y: 4, z: 8, core: 2. Of those that a mesh axis runs over, the one named last changes fastest.
Arguments:
- latents: bfloat16 [32768, 1024], P('seq', 'head'), may hold values from -6 to 6
- known: bfloat16 [32768, 1024], P('seq', 'head'), may hold values from -6 to 6
- seam_mask: int32 [32768], P('seq'), may hold values 0 or 1
- timesteps: int32 [3], replicated, may hold values from 302 to 800, as said below
- block_lists: int32 [256, 6], P('seq'), may hold values from -1 to 255, as said below
- guidance: bfloat16 [2, 1024, 1024], P(None, 'seq'), may hold values from -7 to 7
- modulation_weight: bfloat16 [256, 4, 1024], replicated, may hold values from -0.75 to 0.75
- self_weight: bfloat16 [1024, 3, 1024], P(None, None, 'head')
- self_out_weight: bfloat16 [1024, 1024], P('head'), may hold values from -0.1875 to 0.1875
- cross_weight: bfloat16 [1024, 3, 1024], P(None, None, 'head')
- cross_out_weight: bfloat16 [1024, 1024], P('head'), may hold values from -0.1875 to 0.1875
Outputs:
- denoised: bfloat16 [32768, 1024], P('seq', 'head')
Inputs may be any that keep to these rules, and one draw needn't show every extreme that they name: `block_lists`: row b starts with b itself, followed by distinct blocks of the query's own tile or of the tiles 1 and 4 away on either side along the closed band of 128 tiles; the rest of the row is -1. Some rows hold 6 blocks. `timesteps`: strictly falling.
All inputs are finite; a program needn't handle non-finite values. No bound on the sum of `seam_mask` on one device may be relied on, other than what follows from the above.
Results may differ from a plain program's by a relative error of at most 0.011.
Values may be sent and summed in bfloat16 or wider, within the bound.
A program may use at most 128 MiB of HBM per device.

v0:
```python
import math
import jax
import jax.numpy as jnp
from jax import lax
from jax.sharding import PartitionSpec as P

D = 1024
HEAD_DIM = 64
FREQ = 256
BLOCK = 128
MAXK = 6
ROW = 4
STEPS = 2


def passed_along(block, axis, distance):
    devices = range(lax.axis_size(axis))
    route = [((i - distance) % len(devices), i) for i in devices]
    return lax.ppermute(block, axis, route)


def norm_rows(values):
    values = values.astype(jnp.float32)
    center = values - jnp.mean(values, axis=-1, keepdims=True)
    second = jnp.mean(center * center, axis=-1, keepdims=True)
    return center * lax.rsqrt(second + 1e-06)


def signal_level(moment):
    angle = (moment.astype(jnp.float32) / 1000.0 + 0.008) / 1.008 * (math.pi / 2.0)
    cosine = jnp.cos(angle)
    return cosine * cosine


def modulation_table(moment, modulation_weight):
    half = FREQ // 2
    frequency = jnp.exp(-math.log(10000.0) * jnp.arange(half, dtype=jnp.float32) / half)
    phase = moment.astype(jnp.float32) * frequency
    embed = jnp.concatenate([jnp.cos(phase), jnp.sin(phase)])
    active = jax.nn.silu(embed).astype(jnp.bfloat16)
    width = modulation_weight.shape[2]
    table = jnp.dot(
        active[None, :],
        modulation_weight.reshape(FREQ, 4 * width),
        preferred_element_type=jnp.float32,
    )
    return table.reshape(4, width)


def on_device(
    latents,
    known,
    seam_mask,
    timesteps,
    block_lists,
    guidance,
    modulation_weight,
    self_weight,
    self_out_weight,
    cross_weight,
    cross_out_weight,
):
    cycle_size = lax.axis_size("seq")
    position = lax.axis_index("seq")
    token_count = latents.shape[0]
    local_width = self_weight.shape[2]
    local_heads = local_width // HEAD_DIM
    block_count = token_count // BLOCK
    scale = 1.0 / math.sqrt(HEAD_DIM)
    moves = jnp.array([-ROW, -1, 0, 1, ROW], dtype=jnp.int32)
    tiles = (position + moves) % cycle_size
    names = tiles[:, None] * block_count + jnp.arange(block_count, dtype=jnp.int32)
    listed = jnp.any(block_lists[:, :, None] == names.reshape(-1), axis=1)
    live = jnp.repeat(listed, BLOCK, axis=1)
    self_flat = self_weight.reshape(D, 3 * local_width)
    cross_pair_weight = cross_weight[:, 1:3].reshape(D, 2 * local_width)
    cross_query_weight = cross_weight[:, 0]
    guide_count = guidance.shape[1]
    guide_pairs = []
    for step in range(STEPS):
        guide_in = norm_rows(guidance[step]).astype(jnp.bfloat16)
        paired = jnp.dot(guide_in, cross_pair_weight, preferred_element_type=jnp.float32).astype(
            jnp.bfloat16
        )
        guide_pairs.append(paired.reshape(guide_count, 2, local_width))
    state = latents
    for step in range(STEPS):
        moment = timesteps[step]
        after = timesteps[step + 1]
        table = modulation_table(moment, modulation_weight)
        whole = lax.all_gather(state, "head", axis=1, tiled=True)
        normed = norm_rows(whole)
        mixed_in = (normed * (1.0 + table[1]) + table[0]).astype(jnp.bfloat16)
        plain = normed.astype(jnp.bfloat16)
        projected = jnp.dot(mixed_in, self_flat, preferred_element_type=jnp.float32).astype(
            jnp.bfloat16
        )
        projected = projected.reshape(token_count, 3, local_width)
        query = projected[:, 0]
        pair = projected[:, 1:3]
        window = jnp.concatenate(
            [
                passed_along(pair, "seq", ROW),
                passed_along(pair, "seq", 1),
                pair,
                passed_along(pair, "seq", -1),
                passed_along(pair, "seq", -ROW),
            ],
            axis=0,
        )
        window = window.reshape(-1, 2, local_heads, HEAD_DIM)
        queries = query.reshape(block_count, BLOCK, local_heads, HEAD_DIM)
        scores = (
            jnp.einsum("bqhd,khd->bhqk", queries, window[:, 0], preferred_element_type=jnp.float32)
            * scale
        )
        scores = jnp.where(live[:, None, None, :], scores, -1e30)
        peak = jnp.max(scores, axis=-1, keepdims=True)
        weights = jnp.exp(scores - peak)
        total = jnp.sum(weights, axis=-1)
        rounded = weights.astype(jnp.bfloat16)
        mixed = jnp.einsum(
            "bhqk,khd->bqhd", rounded, window[:, 1], preferred_element_type=jnp.float32
        )
        mixed = mixed / jnp.transpose(total, (0, 2, 1))[:, :, :, None]
        attended = mixed.reshape(token_count, local_width).astype(jnp.bfloat16)
        guide_pair = lax.all_gather(guide_pairs[step], "seq", axis=0, tiled=True)
        every_guide = guide_pair.shape[0]
        guide_keys = guide_pair[:, 0].reshape(every_guide, local_heads, HEAD_DIM)
        guide_values = guide_pair[:, 1].reshape(every_guide, local_heads, HEAD_DIM)
        cross_query = jnp.dot(plain, cross_query_weight, preferred_element_type=jnp.float32).astype(
            jnp.bfloat16
        )
        cross_heads = cross_query.reshape(token_count, local_heads, HEAD_DIM)
        cross_scores = (
            jnp.einsum("qhd,ghd->hqg", cross_heads, guide_keys, preferred_element_type=jnp.float32)
            * scale
        )
        cross_peak = jnp.max(cross_scores, axis=-1, keepdims=True)
        cross_weights = jnp.exp(cross_scores - cross_peak)
        cross_total = jnp.sum(cross_weights, axis=-1)
        cross_rounded = cross_weights.astype(jnp.bfloat16)
        cross_mixed = jnp.einsum(
            "hqg,ghd->qhd", cross_rounded, guide_values, preferred_element_type=jnp.float32
        )
        cross_mixed = cross_mixed / jnp.transpose(cross_total)[:, :, None]
        guided = cross_mixed.reshape(token_count, local_width).astype(jnp.bfloat16)
        partial_value = table[2] * jnp.dot(
            attended, self_out_weight, preferred_element_type=jnp.float32
        )
        partial_value = partial_value + table[3] * jnp.dot(
            guided, cross_out_weight, preferred_element_type=jnp.float32
        )
        noise_pred = lax.psum_scatter(partial_value, "head", scatter_dimension=1, tiled=True)
        level_now = signal_level(moment)
        level_after = signal_level(after)
        current = state.astype(jnp.float32)
        clean = (current - jnp.sqrt(1.0 - level_now) * noise_pred) / jnp.sqrt(level_now)
        moved = jnp.sqrt(level_after) * clean + jnp.sqrt(1.0 - level_after) * noise_pred
        kept = jnp.sqrt(level_after) * known.astype(jnp.float32) + jnp.sqrt(
            1.0 - level_after
        ) * latents.astype(jnp.float32)
        state = jnp.where(seam_mask[:, None] == 1, moved, kept).astype(jnp.bfloat16)
    return state


def solution(mesh):
    in_specs = (
        P("seq", "head"),
        P("seq", "head"),
        P("seq"),
        P(),
        P("seq", None),
        P(None, "seq", None),
        P(),
        P(None, None, "head"),
        P("head", None),
        P(None, None, "head"),
        P("head", None),
    )
    out_specs = P("seq", "head")
    return jax.shard_map(
        on_device, mesh=mesh, in_specs=in_specs, out_specs=out_specs, check_vma=False
    )
```

profile of v0, /device:TPU:1, one launch (start us, length us, event | category | flops | bytes accessed | tf_op | source)
XLA Modules:
  0.0 562.5 jit_solution(7443431622436207543)
XLA Ops:
  6.5 3.2 slice.102
  9.7 3.0 copy.61
  13.1 1.3 convolution_convert_fusion.5
  14.5 2.5 copy.62
  17.0 4.7 copy.39
  21.7 0.6 fusion.153
  23.1 9.4 %all_gather.12 = bf16[256,1024]{1,0:T(8,128)(2,1)S(1)} all-gather(bf16[256,512]{1,0:T(8,128)(2,1)S(1)} %copy-done.6), channel_id=1, replica_groups=mesh['seq'=128,'head'=2] {'head'}, dimensions={1}, use_global_device_ids=true | all-gather | bytes 786432 | tf_op jit(solution)/shard_map/all_gather | solution.py:91
  32.9 0.4 fusion.154
  33.3 4.0 convolution_convert_fusion.1
  37.3 2.3 copy.40
  39.6 1.9 slice.120
  41.5 2.1 collective-permute-start
  43.6 2.9 collective-permute-start.1
  46.5 6.8 %collective-permute-start.3 = (bf16[256,2,512]{0,2,1:T(8,128)(2,1)}, bf16[256,2,512]{0,2,1:T(8,128)(2,1)}, u32[]{:S(2)}, u32[]{:S(2)}) collective-permute-start(bf16[256,2,512]{0,2,1:T(8,128)(2,1)} %slice.120), channel_id=1, source_target_pairs={{8,0},{10,2},{12,4},{14,6},{16,8},{18,10},{20,12},{22,14},{24,16},... | collective-permute-start | bytes 1572872 | tf_op jit(solution)/shard_map/ppermute | solution.py:19
  53.4 2.9 convolution_convert_fusion.4
  56.5 2.6 convolution_convert_fusion.3
  59.4 1.7 slice.123
  61.1 1.7 reshape_squeeze.18
  62.8 1.8 copy.46
  64.6 1.1 constant_dynamic-update-slice_fusion.4
  65.8 1.1 constant_dynamic-update-slice_fusion.3
  66.9 1.1 constant_dynamic-update-slice_fusion.2
  67.9 1.1 constant_dynamic-update-slice_fusion.1
  69.0 1.1 constant_dynamic-update-slice_fusion
  70.1 2.5 fusion.4
  72.6 2.5 fusion
  75.1 2.6 fusion.65
  78.0 1.4 convolution_multiply_fusion.3
  79.5 151.6 %all-gather.3.cloned.1.call-done = bf16[1024,2,512]{2,0,1:T(8,128)(2,1)} async-done(((bf16[8,2,512]{2,0,1:T(8,128)(2,1)}), bf16[1024,2,512]{2,0,1:T(8,128)(2,1)}) %all-gather.3.cloned.1.call-update) | async-done | bytes 2097168 | tf_op jit(solution)/shard_map/all_gather | solution.py:127
  231.1 3.1 fusion.150
  234.2 2.3 copy.45
  236.5 2.3 copy.47
  238.8 2.7 multiply_reduce_fusion.1
  241.5 1.8 fusion.6
  243.3 1.9 fusion.77
  245.3 1.4 fusion.25
  248.1 0.4 fusion.155
  248.5 197.5 %all-gather.5.cloned.1.call-done = bf16[1024,2,512]{2,0,1:T(8,128)(2,1)} async-done(((bf16[8,2,512]{2,0,1:T(8,128)(2,1)}), bf16[1024,2,512]{2,0,1:T(8,128)(2,1)}) %all-gather.5.cloned.1.call-update) | async-done | bytes 2097168 | tf_op jit(solution)/shard_map/all_gather | solution.py:127
  446.0 1.7 fusion.149
  447.7 1.3 copy.52
  449.0 1.3 copy.54
  450.4 24.2 %reduce-scatter.3.cloned.1.call-done = f32[256,512]{1,0:T(8,128)} async-done(((f32[256,1024]{1,0:T(8,128)}), f32[256,512]{1,0:T(8,128)}) %reduce-scatter.3.cloned.1.call-update) | async-done | bytes 524304 | tf_op jit(solution)/shard_map/reduce_scatter | solution.py:154
  474.6 1.3 fusion.84
  475.9 9.4 %all_gather.14 = bf16[256,1024]{1,0:T(8,128)(2,1)S(1)} all-gather(bf16[256,512]{1,0:T(8,128)(2,1)S(1)} %fusion.84), channel_id=1, replica_groups=mesh['seq'=128,'head'=2] {'head'}, dimensions={1}, use_global_device_ids=true | all-gather | bytes 786432 | tf_op jit(solution)/shard_map/all_gather | solution.py:91
  485.8 3.0 convolution_convert_fusion
  489.0 0.8 slice.130
  489.9 1.2 collective-permute-start.4
  491.1 2.0 collective-permute-start.5
  493.1 3.7 collective-permute-start.7
  496.8 1.7 convolution_convert_fusion.2
  498.7 2.6 multiply_reduce_fusion
  501.3 1.8 fusion.8
  503.1 2.6 fusion.71
  506.1 1.1 constant_dynamic-update-slice_fusion.9
  507.1 1.1 constant_dynamic-update-slice_fusion.8
  508.3 1.1 constant_dynamic-update-slice_fusion.6
  509.4 1.1 constant_dynamic-update-slice_fusion.5
  510.5 2.5 fusion.5
  513.0 2.5 fusion.2
  515.5 2.6 fusion.59
  518.4 0.5 convolution_multiply_fusion.1
  518.8 1.5 fusion.24
  521.1 32.3 %reduce-scatter.5.cloned.1.call-done = f32[256,512]{1,0:T(8,128)} async-done(((f32[256,1024]{1,0:T(8,128)}), f32[256,512]{1,0:T(8,128)}) %reduce-scatter.5.cloned.1.call-update) | async-done | bytes 524304 | tf_op jit(solution)/shard_map/reduce_scatter | solution.py:154
  553.4 2.1 fusion.87
  (87 shorter events, 3.8 us)
Async XLA Ops:
  6.5 71.5 %copy-start = (bf16[512,1024]{1,0:T(8,128)(2,1)S(1)}, bf16[512,1024]{1,0:T(8,128)(2,1)}, u32[]{:S(2)}) copy-start(bf16[512,1024]{1,0:T(8,128)(2,1)} %param.20) | copy-start | bytes 3145732
  6.5 6.2 %copy-start.10 = (bf16[2,8,1024]{2,1,0:T(8,128)(2,1)S(1)}, bf16[2,8,1024]{2,1,0:T(8,128)(2,1)}, u32[]{:S(2)}) copy-start(bf16[2,8,1024]{2,1,0:T(8,128)(2,1)} %param.17) | copy-start | bytes 98308
  6.5 224.6 %all-gather.3.cloned.1.call-start = ((), (), s32[]{:S(2)}) async-start(), calls=%async_computation.2 | async-start | bytes 2113536 | tf_op jit(solution)/shard_map/all_gather | solution.py:127
  12.7 1.8 copy-start.1
  14.4 431.6 %all-gather.5.cloned.1.call-start = ((), (), s32[]{:S(2)}) async-start(), calls=%async_computation.4 | async-start | bytes 2113536 | tf_op jit(solution)/shard_map/all_gather | solution.py:127
  16.9 4.8 copy-start.13
  16.9 6.1 %copy-start.6 = (bf16[256,512]{1,0:T(8,128)(2,1)S(1)}, bf16[256,512]{1,0:T(8,128)(2,1)}, u32[]{:S(2)}) copy-start(bf16[256,512]{1,0:T(8,128)(2,1)} %param.12) | copy-start | bytes 786436
  32.5 0.9 copy-start.2
  37.3 21.8 %copy-start.16 = (s32[5]{0:T(128)S(1)}, s32[5]{0:T(128)}, u32[]{:S(2)}) copy-start(s32[5]{0:T(128)} %constant.85.clone) | copy-start | bytes 64
  37.3 21.9 %copy-start.14 = (s32[2,6]{1,0:T(2,128)S(1)}, s32[2,6]{1,0:T(2,128)}, u32[]{:S(2)}) copy-start(s32[2,6]{1,0:T(2,128)} %param.16) | copy-start | bytes 148
  41.5 23.1 %collective-permute-start = (bf16[256,2,512]{0,2,1:T(8,128)(2,1)}, bf16[256,2,512]{0,2,1:T(8,128)(2,1)}, u32[]{:S(2)}, u32[]{:S(2)}) collective-permute-start(bf16[256,2,512]{0,2,1:T(8,128)(2,1)} %slice.120), channel_id=1, source_target_pairs={{248,0},{250,2},{252,4},{254,6},{0,8},{2,10},{4,12},{6,14},{8,16},... | collective-permute-start | bytes 1572872 | tf_op jit(solution)/shard_map/ppermute | solution.py:19
  43.6 22.1 %collective-permute-start.1 = (bf16[256,2,512]{0,2,1:T(8,128)(2,1)}, bf16[256,2,512]{0,2,1:T(8,128)(2,1)}, u32[]{:S(2)}, u32[]{:S(2)}) collective-permute-start(bf16[256,2,512]{0,2,1:T(8,128)(2,1)} %slice.120), channel_id=1, source_target_pairs={{254,0},{0,2},{2,4},{4,6},{6,8},{8,10},{10,12},{12,14},{14,16},{16... | collective-permute-start | bytes 1572872 | tf_op jit(solution)/shard_map/ppermute | solution.py:19
  46.5 21.4 %collective-permute-start.2 = (bf16[256,2,512]{0,2,1:T(8,128)(2,1)}, bf16[256,2,512]{0,2,1:T(8,128)(2,1)}, u32[]{:S(2)}, u32[]{:S(2)}) collective-permute-start(bf16[256,2,512]{0,2,1:T(8,128)(2,1)} %slice.120), channel_id=1, source_target_pairs={{2,0},{4,2},{6,4},{8,6},{10,8},{12,10},{14,12},{16,14},{18,16},{20... | collective-permute-start | bytes 1572872 | tf_op jit(solution)/shard_map/ppermute | solution.py:19
  46.5 22.5 %collective-permute-start.3 = (bf16[256,2,512]{0,2,1:T(8,128)(2,1)}, bf16[256,2,512]{0,2,1:T(8,128)(2,1)}, u32[]{:S(2)}, u32[]{:S(2)}) collective-permute-start(bf16[256,2,512]{0,2,1:T(8,128)(2,1)} %slice.120), channel_id=1, source_target_pairs={{8,0},{10,2},{12,4},{14,6},{16,8},{18,10},{20,12},{22,14},{24,16},... | collective-permute-start | bytes 1572872 | tf_op jit(solution)/shard_map/ppermute | solution.py:19
  56.3 418.3 %reduce-scatter.3.cloned.1.call-start = ((), (), s32[]{:S(2)}) async-start(), calls=%async_computation.3 | async-start | bytes 1572864 | tf_op jit(solution)/shard_map/reduce_scatter | solution.py:154
  64.6 5.5 copy-start.11
  241.5 1.8 copy-start.9
  243.3 2.0 copy-start.3
  243.3 2.0 copy-start.4
  245.3 2.8 copy-start.15
  246.8 306.7 %reduce-scatter.5.cloned.1.call-start = ((), (), s32[]{:S(2)}) async-start(), calls=%async_computation.5 | async-start | bytes 1572864 | tf_op jit(solution)/shard_map/reduce_scatter | solution.py:154
  475.9 9.8 %copy-start.7 = (bf16[256,512]{1,0:T(8,128)(2,1)}, bf16[256,512]{1,0:T(8,128)(2,1)S(1)}, u32[]{:S(2)}) copy-start(bf16[256,512]{1,0:T(8,128)(2,1)S(1)} %fusion.84) | copy-start | bytes 786436
  489.9 16.2 %collective-permute-start.4 = (bf16[256,2,512]{0,2,1:T(8,128)(2,1)}, bf16[256,2,512]{0,2,1:T(8,128)(2,1)}, u32[]{:S(2)}, u32[]{:S(2)}) collective-permute-start(bf16[256,2,512]{0,2,1:T(8,128)(2,1)} %slice.130), channel_id=1, source_target_pairs={{248,0},{250,2},{252,4},{254,6},{0,8},{2,10},{4,12},{6,14},{8,16},... | collective-permute-start | bytes 1572872 | tf_op jit(solution)/shard_map/ppermute | solution.py:19
  491.1 16.1 %collective-permute-start.5 = (bf16[256,2,512]{0,2,1:T(8,128)(2,1)}, bf16[256,2,512]{0,2,1:T(8,128)(2,1)}, u32[]{:S(2)}, u32[]{:S(2)}) collective-permute-start(bf16[256,2,512]{0,2,1:T(8,128)(2,1)} %slice.130), channel_id=1, source_target_pairs={{254,0},{0,2},{2,4},{4,6},{6,8},{8,10},{10,12},{12,14},{14,16},{16... | collective-permute-start | bytes 1572872 | tf_op jit(solution)/shard_map/ppermute | solution.py:19
  493.1 15.2 %collective-permute-start.6 = (bf16[256,2,512]{0,2,1:T(8,128)(2,1)}, bf16[256,2,512]{0,2,1:T(8,128)(2,1)}, u32[]{:S(2)}, u32[]{:S(2)}) collective-permute-start(bf16[256,2,512]{0,2,1:T(8,128)(2,1)} %slice.130), channel_id=1, source_target_pairs={{2,0},{4,2},{6,4},{8,6},{10,8},{12,10},{14,12},{16,14},{18,16},{20... | collective-permute-start | bytes 1572872 | tf_op jit(solution)/shard_map/ppermute | solution.py:19
  493.1 16.3 %collective-permute-start.7 = (bf16[256,2,512]{0,2,1:T(8,128)(2,1)}, bf16[256,2,512]{0,2,1:T(8,128)(2,1)}, u32[]{:S(2)}, u32[]{:S(2)}) collective-permute-start(bf16[256,2,512]{0,2,1:T(8,128)(2,1)} %slice.130), channel_id=1, source_target_pairs={{8,0},{10,2},{12,4},{14,6},{16,8},{18,10},{20,12},{22,14},{24,16},... | collective-permute-start | bytes 1572872 | tf_op jit(solution)/shard_map/ppermute | solution.py:19
  501.3 1.8 copy-start.8
  515.4 3.4 copy-start.5
  515.4 3.4 copy-start.12
Sparse Core Ops, SparseCore 0:
  14.5 216.5 all-gather.2
  233.0 212.9 all-gather.4
  448.5 26.0 reduce-scatter.2
  520.5 32.9 reduce-scatter.4
where the time goes:
time: 570 us; the launch traced here: 562 us
  waiting for transfers between devices  406 us (71%)
  local copies, waits for them, and re-layouts  47.3 us (8%)
  matrix products  41.1 us (7%)
  starting transfers between devices  19.3 us (3%)
  blocking collectives  18.8 us (3%)
  between operations  16.4 us (3%)
  other arithmetic  13.6 us (2%)
    all_gather x2, waiting for transfers between devices, on_device(): guide_pair = lax.all_gather(guide_pairs[step], 'seq', axis=0, tiled=True)  349 us
    reduce_scatter x2, waiting for transfers between devices, on_device(): lax.psum_scatter(partial_value, 'head', scatter_dimension=1, tiled=True)  56.5 us
    ppermute x8, starting transfers between devices, passed_along(): return lax.ppermute(block, axis, route)  18.8 us
    all_gather x2, blocking collectives, on_device(): whole = lax.all_gather(state, 'head', axis=1, tiled=True)  18.8 us
    unnamed x47, local copies, waits for them, and re-layouts  18 us
  transfers between devices with their start and end apart: 12, of which 5 were waited for; matrix products, arithmetic and copies ran while one was open for 13% of the time, Pallas kernels for 0%

commit v1 on v0

--- a/solution.py
+++ b/solution.py
@@ -88,7 +88,9 @@
         moment = timesteps[step]
         after = timesteps[step + 1]
         table = modulation_table(moment, modulation_weight)
-        whole = lax.all_gather(state, "head", axis=1, tiled=True)
+        whole = jnp.concatenate(
+            lax.all_to_all(jnp.stack([state] * lax.axis_size("head")), "head", 0, 0), axis=1
+        )
         normed = norm_rows(whole)
         mixed_in = (normed * (1.0 + table[1]) + table[0]).astype(jnp.bfloat16)
         plain = normed.astype(jnp.bfloat16)

time: 570 us -> 590 us (1.035)
  blocking collectives: 18.8 us -> 0 us
  waiting for transfers between devices: 406 us -> 423 us
  starting transfers between devices: 19.3 us -> 26.8 us
  other arithmetic: 13.6 us -> 20.5 us
    all_gather x2, waiting for transfers between devices: 349 us -> 369 us  [on_device(): guide_pair = lax.all_gather(guide_pairs[step], 'seq', axis=0, tiled=True)]
    all_gather x2 -> x0, blocking collectives: 18.8 us -> none  [on_device(): whole = lax.all_gather(state, 'head', axis=1, tiled=True)]
    all_to_all x0 -> x2, starting transfers between devices: none -> 8.33 us  [on_device(): lax.all_to_all(jnp.stack([state] * lax.axis_size('head')), 'head', 0, 0)]
    reduce_scatter x2, waiting for transfers between devices: 56.5 us -> 49.9 us  [on_device(): lax.psum_scatter(partial_value, 'head', scatter_dimension=1, tiled=True)]
    unnamed x47 -> x48, local copies, waits for them, and re-layouts: 18 us -> 19.1 us
  transfers between devices with their start and end apart: 12 -> 14, of which waited for: 5 -> 5; matrix products, arithmetic and copies ran while one was open for 13% -> 13% of each run, Pallas kernels for 0% -> 0%
where the time goes in v1:
time: 590 us; the launch traced here: 582 us
  waiting for transfers between devices  423 us (72%)
  local copies, waits for them, and re-layouts  53 us (9%)
  matrix products  42.3 us (7%)
  starting transfers between devices  26.8 us (5%)
  other arithmetic  20.5 us (3%)
  between operations  16.3 us (3%)
    all_gather x2, waiting for transfers between devices, on_device(): guide_pair = lax.all_gather(guide_pairs[step], 'seq', axis=0, tiled=True)  369 us
    reduce_scatter x2, waiting for transfers between devices, on_device(): lax.psum_scatter(partial_value, 'head', scatter_dimension=1, tiled=True)  49.9 us
    unnamed x48, local copies, waits for them, and re-layouts  19.1 us
    ppermute x8, starting transfers between devices, passed_along(): return lax.ppermute(block, axis, route)  18.2 us
  transfers between devices with their start and end apart: 14, of which 5 were waited for; matrix products, arithmetic and copies ran while one was open for 13% of the time, Pallas kernels for 0%

profile of v1, /device:TPU:1, one launch (start us, length us, event | category | flops | bytes accessed | tf_op | source)
XLA Modules:
  0.0 581.9 jit_solution(12263355247650020385)
XLA Ops:
  6.5 1.2 copy.42
  8.6 4.8 all-to-all-start
  13.4 3.1 slice.127
  16.5 3.0 copy.67
  19.9 1.3 convolution_convert_fusion.5
  22.0 2.5 copy.68
  25.7 4.7 copy.43
  30.4 1.2 convert_reduce_fusion.1
  31.6 1.2 fusion.53
  32.9 2.2 fusion.46
  35.0 3.9 convolution_convert_fusion.1
  39.0 2.3 copy.44
  41.2 1.9 slice.146
  43.2 1.6 collective-permute-start
  44.8 2.1 collective-permute-start.1
  47.1 7.0 %collective-permute-start.3 = (bf16[256,2,512]{0,2,1:T(8,128)(2,1)}, bf16[256,2,512]{0,2,1:T(8,128)(2,1)}, u32[]{:S(2)}, u32[]{:S(2)}) collective-permute-start(bf16[256,2,512]{0,2,1:T(8,128)(2,1)} %slice.146), channel_id=1, source_target_pairs={{8,0},{10,2},{12,4},{14,6},{16,8},{18,10},{20,12},{22,14},{24,16},... | collective-permute-start | bytes 1572872 | tf_op jit(solution)/shard_map/ppermute | solution.py:19
  54.1 2.6 convolution_convert_fusion.3
  58.4 1.1 copy.50
  59.5 3.9 collective-permute-done
  64.5 1.1 constant_dynamic-update-slice_fusion.3
  65.6 1.1 constant_dynamic-update-slice_fusion.2
  66.7 1.1 constant_dynamic-update-slice_fusion.1
  67.8 1.1 constant_dynamic-update-slice_fusion
  68.8 2.5 fusion.4
  71.4 2.5 fusion
  73.8 2.6 fusion.65
  76.7 1.5 convolution_multiply_fusion.3
  78.2 160.8 %all-gather.3.cloned.1.call-done = bf16[1024,2,512]{2,0,1:T(8,128)(2,1)} async-done(((bf16[8,2,512]{2,0,1:T(8,128)(2,1)}), bf16[1024,2,512]{2,0,1:T(8,128)(2,1)}) %all-gather.3.cloned.1.call-update) | async-done | bytes 2097168 | tf_op jit(solution)/shard_map/all_gather | solution.py:129
  239.0 3.1 fusion.136
  242.1 2.3 copy.49
  244.3 2.3 copy.51
  246.6 2.6 multiply_reduce_fusion.1
  249.2 1.8 fusion.6
  251.1 1.9 fusion.77
  253.1 1.5 fusion.25
  254.8 2.9 convolution_convert_fusion.4
  259.2 22.1 %reduce-scatter.3.cloned.1.call-done = f32[256,512]{1,0:T(8,128)} async-done(((f32[256,1024]{1,0:T(8,128)}), f32[256,512]{1,0:T(8,128)}) %reduce-scatter.3.cloned.1.call-update) | async-done | bytes 524304 | tf_op jit(solution)/shard_map/reduce_scatter | solution.py:156
  281.3 1.3 fusion.84
  283.5 3.5 all-to-all-start.1
  287.0 208.3 %all-gather.5.cloned.1.call-done = bf16[1024,2,512]{2,0,1:T(8,128)(2,1)} async-done(((bf16[8,2,512]{2,0,1:T(8,128)(2,1)}), bf16[1024,2,512]{2,0,1:T(8,128)(2,1)}) %all-gather.5.cloned.1.call-update) | async-done | bytes 2097168 | tf_op jit(solution)/shard_map/all_gather | solution.py:129
  495.3 2.7 fusion.135
  498.0 2.3 copy.57
  500.3 1.3 copy.60
  502.0 1.1 fusion.92
  503.4 3.8 convolution_convert_fusion
  507.2 1.5 copy.53
  509.5 2.4 collective-permute-start.5
  511.9 5.0 collective-permute-start.7
  516.9 2.1 copy.58
  519.0 2.5 convolution_convert_fusion.2
  521.5 1.8 copy.59
  523.3 2.3 multiply_reduce_fusion
  525.7 1.8 fusion.8
  527.5 2.6 fusion.71
  530.2 1.1 constant_dynamic-update-slice_fusion.9
  531.3 1.1 constant_dynamic-update-slice_fusion.8
  532.4 1.1 constant_dynamic-update-slice_fusion.6
  533.5 1.1 constant_dynamic-update-slice_fusion.5
  534.6 2.5 fusion.5
  537.1 2.5 fusion.2
  539.6 2.6 fusion.59
  543.0 1.5 fusion.24
  545.3 27.8 %reduce-scatter.5.cloned.1.call-done = f32[256,512]{1,0:T(8,128)} async-done(((f32[256,1024]{1,0:T(8,128)}), f32[256,512]{1,0:T(8,128)}) %reduce-scatter.5.cloned.1.call-update) | async-done | bytes 524304 | tf_op jit(solution)/shard_map/reduce_scatter | solution.py:156
  573.1 2.0 fusion.87
  (100 shorter events, 10.0 us)
Async XLA Ops:
  6.5 70.2 %copy-start = (bf16[512,1024]{1,0:T(8,128)(2,1)S(1)}, bf16[512,1024]{1,0:T(8,128)(2,1)}, u32[]{:S(2)}) copy-start(bf16[512,1024]{1,0:T(8,128)(2,1)} %param.20) | copy-start | bytes 3145732
  8.6 21.8 %all-to-all-start = ((bf16[2,256,512]{1,2,0:T(8,128)(2,1)}), bf16[2,256,512]{1,2,0:T(8,128)(2,1)}, u32[]{:S(2)}, u32[]{:S(2)}) async-start(bf16[2,256,512]{1,2,0:T(8,128)(2,1)} %pad_maximum_fusion), calls=%async_computation | async-start | bytes 1048576 | tf_op jit(solution)/shard_map/all_to_all | solution.py:92
  13.4 6.1 %copy-start.10 = (bf16[2,8,1024]{2,1,0:T(8,128)(2,1)S(1)}, bf16[2,8,1024]{2,1,0:T(8,128)(2,1)}, u32[]{:S(2)}) copy-start(bf16[2,8,1024]{2,1,0:T(8,128)(2,1)} %param.17) | copy-start | bytes 98308
  13.4 225.6 %all-gather.3.cloned.1.call-start = ((), (), s32[]{:S(2)}) async-start(), calls=%async_computation.4 | async-start | bytes 2113536 | tf_op jit(solution)/shard_map/all_gather | solution.py:129
  16.5 4.8 copy-start.13
  19.5 2.4 copy-start.1
  19.5 5.6 copy-start.16
  21.2 260.0 %reduce-scatter.3.cloned.1.call-start = ((), (), s32[]{:S(2)}) async-start(), calls=%async_computation.5 | async-start | bytes 1572864 | tf_op jit(solution)/shard_map/reduce_scatter | solution.py:156
  35.0 9.7 %copy-start.14 = (s32[2,6]{1,0:T(2,128)S(1)}, s32[2,6]{1,0:T(2,128)}, u32[]{:S(2)}) copy-start(s32[2,6]{1,0:T(2,128)} %param.16) | copy-start | bytes 148
  43.2 20.2 %collective-permute-start = (bf16[256,2,512]{0,2,1:T(8,128)(2,1)}, bf16[256,2,512]{0,2,1:T(8,128)(2,1)}, u32[]{:S(2)}, u32[]{:S(2)}) collective-permute-start(bf16[256,2,512]{0,2,1:T(8,128)(2,1)} %slice.146), channel_id=1, source_target_pairs={{248,0},{250,2},{252,4},{254,6},{0,8},{2,10},{4,12},{6,14},{8,16},... | collective-permute-start | bytes 1572872 | tf_op jit(solution)/shard_map/ppermute | solution.py:19
  44.8 19.7 %collective-permute-start.1 = (bf16[256,2,512]{0,2,1:T(8,128)(2,1)}, bf16[256,2,512]{0,2,1:T(8,128)(2,1)}, u32[]{:S(2)}, u32[]{:S(2)}) collective-permute-start(bf16[256,2,512]{0,2,1:T(8,128)(2,1)} %slice.146), channel_id=1, source_target_pairs={{254,0},{0,2},{2,4},{4,6},{6,8},{8,10},{10,12},{12,14},{14,16},{16... | collective-permute-start | bytes 1572872 | tf_op jit(solution)/shard_map/ppermute | solution.py:19
  47.0 19.6 %collective-permute-start.2 = (bf16[256,2,512]{0,2,1:T(8,128)(2,1)}, bf16[256,2,512]{0,2,1:T(8,128)(2,1)}, u32[]{:S(2)}, u32[]{:S(2)}) collective-permute-start(bf16[256,2,512]{0,2,1:T(8,128)(2,1)} %slice.146), channel_id=1, source_target_pairs={{2,0},{4,2},{6,4},{8,6},{10,8},{12,10},{14,12},{16,14},{18,16},{20... | collective-permute-start | bytes 1572872 | tf_op jit(solution)/shard_map/ppermute | solution.py:19
  47.1 20.6 %collective-permute-start.3 = (bf16[256,2,512]{0,2,1:T(8,128)(2,1)}, bf16[256,2,512]{0,2,1:T(8,128)(2,1)}, u32[]{:S(2)}, u32[]{:S(2)}) collective-permute-start(bf16[256,2,512]{0,2,1:T(8,128)(2,1)} %slice.146), channel_id=1, source_target_pairs={{8,0},{10,2},{12,4},{14,6},{16,8},{18,10},{20,12},{22,14},{24,16},... | collective-permute-start | bytes 1572872 | tf_op jit(solution)/shard_map/ppermute | solution.py:19
  59.5 9.3 %copy-start.11 = (bf16[2,128,8,64]{1,0,3,2:T(2,128)(2,1)S(1)}, bf16[2,128,8,64]{1,0,3,2:T(2,128)(2,1)}, u32[]{:S(2)}) copy-start(bf16[2,128,8,64]{1,0,3,2:T(2,128)(2,1)} %reshape_squeeze.18) | copy-start | bytes 786436
  249.2 1.8 copy-start.8
  251.1 2.0 copy-start.2
  251.1 2.0 copy-start.3
  253.1 6.1 %copy-start.15 = (s32[256]{0:T(256)S(1)}, s32[256]{0:T(256)}, u32[]{:S(2)}) copy-start(s32[256]{0:T(256)} %param.14) | copy-start | bytes 3076
  253.1 28.2 %copy-start.6 = (bf16[256,512]{1,0:T(8,128)(2,1)S(1)}, bf16[256,512]{1,0:T(8,128)(2,1)}, u32[]{:S(2)}) copy-start(bf16[256,512]{1,0:T(8,128)(2,1)} %param.12) | copy-start | bytes 786436
  254.6 240.7 %all-gather.5.cloned.1.call-start = ((), (), s32[]{:S(2)}) async-start(), calls=%async_computation.6 | async-start | bytes 2113536 | tf_op jit(solution)/shard_map/all_gather | solution.py:129
  283.5 218.1 %all-to-all-start.1 = ((bf16[2,256,512]{2,1,0:T(8,128)(2,1)}), bf16[2,256,512]{2,1,0:T(8,128)(2,1)S(1)}, u32[]{:S(2)}, u32[]{:S(2)}) async-start(bf16[2,256,512]{2,1,0:T(8,128)(2,1)} %pad_maximum_fusion.1), calls=%async_computation.2 | async-start | bytes 1048576 | tf_op jit(solution)/shard_map/all_to_all | solution.py:92
  287.0 286.2 %reduce-scatter.5.cloned.1.call-start = ((), (), s32[]{:S(2)}) async-start(), calls=%async_computation.7 | async-start | bytes 1572864 | tf_op jit(solution)/shard_map/reduce_scatter | solution.py:156
  507.2 16.2 %copy-start.5 = (bf16[1024,1,512]{0,2,1:T(8,128)(2,1)S(1)}, bf16[1024,1,512]{0,2,1:T(8,128)(2,1)}, u32[]{:S(2)}) copy-start(bf16[1024,1,512]{0,2,1:T(8,128)(2,1)} %copy.60) | copy-start | bytes 3145732
  509.5 20.7 %collective-permute-start.4 = (bf16[256,2,512]{0,2,1:T(8,128)(2,1)}, bf16[256,2,512]{0,2,1:T(8,128)(2,1)}, u32[]{:S(2)}, u32[]{:S(2)}) collective-permute-start(bf16[256,2,512]{0,2,1:T(8,128)(2,1)} %slice.156), channel_id=1, source_target_pairs={{248,0},{250,2},{252,4},{254,6},{0,8},{2,10},{4,12},{6,14},{8,16},... | collective-permute-start | bytes 1572872 | tf_op jit(solution)/shard_map/ppermute | solution.py:19
  509.5 21.8 %collective-permute-start.5 = (bf16[256,2,512]{0,2,1:T(8,128)(2,1)}, bf16[256,2,512]{0,2,1:T(8,128)(2,1)}, u32[]{:S(2)}, u32[]{:S(2)}) collective-permute-start(bf16[256,2,512]{0,2,1:T(8,128)(2,1)} %slice.156), channel_id=1, source_target_pairs={{254,0},{0,2},{2,4},{4,6},{6,8},{8,10},{10,12},{12,14},{14,16},{16... | collective-permute-start | bytes 1572872 | tf_op jit(solution)/shard_map/ppermute | solution.py:19
  511.9 20.5 %collective-permute-start.6 = (bf16[256,2,512]{0,2,1:T(8,128)(2,1)}, bf16[256,2,512]{0,2,1:T(8,128)(2,1)}, u32[]{:S(2)}, u32[]{:S(2)}) collective-permute-start(bf16[256,2,512]{0,2,1:T(8,128)(2,1)} %slice.156), channel_id=1, source_target_pairs={{2,0},{4,2},{6,4},{8,6},{10,8},{12,10},{14,12},{16,14},{18,16},{20... | collective-permute-start | bytes 1572872 | tf_op jit(solution)/shard_map/ppermute | solution.py:19
  511.9 21.6 %collective-permute-start.7 = (bf16[256,2,512]{0,2,1:T(8,128)(2,1)}, bf16[256,2,512]{0,2,1:T(8,128)(2,1)}, u32[]{:S(2)}, u32[]{:S(2)}) collective-permute-start(bf16[256,2,512]{0,2,1:T(8,128)(2,1)} %slice.156), channel_id=1, source_target_pairs={{8,0},{10,2},{12,4},{14,6},{16,8},{18,10},{20,12},{22,14},{24,16},... | collective-permute-start | bytes 1572872 | tf_op jit(solution)/shard_map/ppermute | solution.py:19
  525.7 1.8 copy-start.7
  539.6 3.4 copy-start.4
  539.6 3.4 copy-start.12
  542.2 30.9 %copy-start.9 = (bf16[256,512]{1,0:T(8,128)(2,1)S(1)}, bf16[256,512]{1,0:T(8,128)(2,1)}, u32[]{:S(2)}) copy-start(bf16[256,512]{1,0:T(8,128)(2,1)} %param.13) | copy-start | bytes 786436
Sparse Core Ops, SparseCore 0:
  21.4 217.5 all-gather.2
  254.7 26.5 reduce-scatter.2
  283.3 211.9 all-gather.4
  544.6 28.4 reduce-scatter.4
